TPU v7x, 512 devices: a whole 4x8x8 slice. The times are simulated.
512 devices in a mesh: blk: 8 (over y_lo, core), leaf: 64 (over z, y_hi, x).
Axes of the slice: x: 4, y: 8 (y_hi: 2, y_lo: 4; y = y_hi * 4 + y_lo), z: 8, core: 2. Of those that a mesh axis runs over, the one named last changes fastest.
Arguments:
- positions: float32 [3, 64, 8, 128], P(None, 'leaf', 'blk'), may hold values from 0 to 32, as said below
- panel_areas: float32 [64, 8, 128], P('leaf', 'blk'), may hold values from 0.5 to 2
- probe_cols: bfloat16 [576, 64, 8, 128], P(None, 'leaf', 'blk'), may hold values from -5 to 5
- full_sketch: bfloat16 [576, 64, 8, 128], P(None, 'leaf', 'blk'), may hold values from -3 to 3
- tree_order: int32 [64, 8, 128], P('leaf', 'blk'), may hold values from 0 to 127, each once within a row
- leaf_basis: bfloat16 [64, 8, 128, 512], P('leaf', 'blk'), may hold values from -0.1875 to 0.1875
- transfer_mats: bfloat16 [64, 3, 512, 512], P('leaf'), may hold values from -0.1875 to 0.1875
Outputs:
- offdiag_sketch: bfloat16 [576, 64, 8, 128], P(None, 'leaf', 'blk')
- nested_sketch: float32 [64, 2, 576, 512], P('leaf')
Inputs may be any that keep to these rules, and one draw needn't show every extreme that they name: `positions`: each leaf's panel centres lie on a surface patch of 32 by 32 mean panel widths. `tree_order`: along the last dimension, each row names every one of the 128 panels of its block once.
All inputs are finite; a program needn't handle non-finite values.
Results may differ from a plain program's by a relative error of at most 0.0046.
Values sent between devices are 32-bit elements; how exact they have to be, the bound alone decides.
No kernel may reach another device: no remote copies, remote signals or barrier semaphores. Data moves between devices by JAX's collectives and lax.ppermute only.
A program may use at most 64 MiB of HBM per device.

v0:
```python
import math
import jax
import jax.numpy as jnp
from jax import lax
from jax.sharding import PartitionSpec as P

inv_four_pi = 1.0 / (4.0 * math.pi)


def partner(value, axis, bit):
    mask = 2**bit
    pairs = [(source, source ^ mask) for source in range(lax.axis_size(axis))]
    return lax.ppermute(value, axis, pairs)


def kernel_tile(target_pos, target_area, source_pos, source_area):
    distance = jnp.zeros((target_pos.shape[1], source_pos.shape[1]), jnp.float32)
    for component in range(3):
        gap = target_pos[component][:, None] - source_pos[component][None, :]
        distance = distance + gap * gap
    soft = distance + 0.5 * (target_area[:, None] + source_area[None, :])
    return (inv_four_pi * lax.rsqrt(soft)).astype(jnp.bfloat16)


def target_blocks(target_pos, target_area):
    panels = target_pos.shape[1]
    block_size = min(512, panels)
    block_count = panels // block_size
    pos_blocks = jnp.transpose(target_pos.reshape(3, block_count, block_size), (1, 0, 2))
    return (pos_blocks, target_area.reshape(block_count, block_size))


def near_block(target_pos, target_area, source_pos, source_area, source_scaled):
    pos_blocks, area_blocks = target_blocks(target_pos, target_area)

    def one_block(entry):
        block_pos, block_area = entry
        kernel = kernel_tile(block_pos, block_area, source_pos, source_area)
        return lax.dot_general(
            source_scaled, kernel, (((1,), (1,)), ((), ())), preferred_element_type=jnp.float32
        )

    sums = lax.map(one_block, (pos_blocks, area_blocks))
    return jnp.transpose(sums, (1, 0, 2)).reshape(source_scaled.shape[0], target_pos.shape[1])


def project(current, level_mat):
    return jnp.dot(current, level_mat.astype(jnp.float32), precision=lax.Precision.HIGHEST)


def climb_both(sketch, probes, level_mats):
    for tree_level in range(level_mats.shape[0]):
        sketch_proj = project(sketch, level_mats[tree_level])
        probe_proj = project(probes, level_mats[tree_level])
        other_sketch, other_probe = partner((sketch_proj, probe_proj), "leaf", tree_level)
        sketch = sketch_proj + other_sketch
        probes = probe_proj + other_probe
    return (sketch, probes)


def shards(positions, panel_areas, probe_cols, full_sketch, tree_order, leaf_basis, transfer_mats):
    panels = positions.shape[3]
    probe_count = probe_cols.shape[0]
    basis_width = leaf_basis.shape[3]
    level_count = transfer_mats.shape[1]
    coords = positions.reshape(3, panels)
    area_row = panel_areas.reshape(1, panels)
    probe_flat = probe_cols.reshape(probe_count, panels)
    scaled = (area_row * probe_flat.astype(jnp.float32)).astype(jnp.bfloat16)
    sorting = tree_order.reshape(panels)
    basis_flat = leaf_basis.reshape(panels, basis_width)
    level_mats = transfer_mats.reshape(level_count, basis_width, basis_width)
    probe_part = jnp.dot(
        jnp.take(probe_flat, sorting, axis=1), basis_flat, preferred_element_type=jnp.float32
    )
    outgoing = jnp.concatenate([coords, area_row, scaled.astype(jnp.float32)], axis=0)
    piece = lax.all_gather(outgoing, "blk", axis=1, tiled=True)
    near_sum = near_block(coords, area_row[0], piece[:3], piece[3], piece[4:].astype(jnp.bfloat16))
    offdiag = (full_sketch.reshape(probe_count, panels).astype(jnp.float32) - near_sum).astype(
        jnp.bfloat16
    )
    sketch_part = jnp.dot(
        jnp.take(offdiag, sorting, axis=1), basis_flat, preferred_element_type=jnp.float32
    )
    sketch_sum, probe_sum = lax.psum((sketch_part, probe_part), "blk")
    sketch_top, probe_top = climb_both(sketch_sum, probe_sum, level_mats)
    nested = jnp.stack([sketch_top, probe_top], axis=0)[None]
    return (offdiag.reshape(probe_count, 1, 1, panels), nested)


def solution(mesh):
    in_specs = (
        P(None, "leaf", "blk", None),
        P("leaf", "blk", None),
        P(None, "leaf", "blk", None),
        P(None, "leaf", "blk", None),
        P("leaf", "blk", None),
        P("leaf", "blk", None, None),
        P("leaf", None, None, None),
    )
    out_specs = (P(None, "leaf", "blk", None), P("leaf", None, None, None))
    return jax.shard_map(shards, mesh=mesh, in_specs=in_specs, out_specs=out_specs, check_vma=False)
```

profile of v0, /device:TPU:25, one launch (start us, length us, event | category | flops | bytes accessed | tf_op | source)
XLA Modules:
  0.0 356.3 jit_solution(13410690366226778184)
XLA Ops:
  7.2 0.0 copy-start
  7.2 0.0 copy-start.6
  7.2 0.0 all-gather.2.cloned.1.call-start
  7.2 0.8 copy.15
  8.0 0.8 copy.13
  8.8 1.1 copy.14
  9.8 0.7 fusion.36
  10.6 0.0 copy-start.4
  10.6 0.9 pad_maximum_fusion
  11.5 0.0 all-gather.2.cloned.1.call-update
  11.6 0.0 all-reduce.3.cloned.1.call-start
  11.6 0.0 copy-done.6
  11.6 0.9 gather_fusion.1
  12.5 0.0 copy-done.4
  12.6 0.0 copy-done
  12.6 1.4 fusion.37
  14.0 44.9 %all-gather.2.cloned.1.call-done = f32[580,1024]{0,1:T(8,128)} async-done(((f32[580,128]{0,1:T(8,128)}), f32[580,1024]{0,1:T(8,128)}) %all-gather.2.cloned.1.call-update) | async-done | bytes 2375696 | tf_op jit(solution)/shard_map/all_gather | solution.py:77
  58.9 2.8 slice_reduce_fusion.3
  61.8 0.0 copy-done.3
  61.8 0.0 copy-done.5
  61.8 3.6 %fusion.23 = (bf16[576,1,1,128]{3,0,2,1:T(8,128)(2,1)}, f32[576,128]{1,0:T(8,128)S(1)}) fusion(bf16[576,1,1,128]{3,0,2,1:T(8,128)(2,1)S(1)} %copy-done.3, f32[1024]{0:T(1024)S(1)} %get-tuple-element.18, f32[128]{0:T(128)S(1)} %bitcast.61, f32[1024]{0:T(1024)S(1)} %get-tuple-element.19, f32[128]{0:T(128)S(1)} %get-tuple-element.31, ...), kind=kOutput, calls=%fused_computation.38 | convolution fusion | flops 152920064 | bytes 1918976 | tf_op jit(solution)/shard_map/while/body/eval_jaxpr/dot_general | solution.py:39
  65.4 0.2 copy.16
  65.6 0.9 gather_fusion
  66.5 1.4 fusion.39
  67.9 0.0 all-reduce.3.cloned.1.call-update
  67.9 87.3 %all-reduce.3.cloned.1.call-done = (f32[576,512]{1,0:T(8,128)}, f32[576,512]{1,0:T(8,128)}) async-done(((f32[576,512]{1,0:T(8,128)}, f32[576,512]{1,0:T(8,128)}), (f32[576,512]{1,0:T(8,128)}, f32[576,512]{1,0:T(8,128)})) %all-reduce.3.cloned.1.call-update) | async-done | bytes 2359312 | tf_op jit(solution)/shard_map/psum | solution.py:85
  155.2 0.0 copy-done.1
  155.2 2.5 fusion.15
  157.7 3.1 collective-permute-start
  160.8 1.1 fusion.13
  161.9 2.2 collective-permute-start.3
  164.1 23.5 %collective-permute-done = f32[576,512]{1,0:T(8,128)S(1)} collective-permute-done((f32[576,512]{1,0:T(8,128)S(1)}, f32[576,512]{1,0:T(8,128)S(1)}, u32[]{:S(2)}, u32[]{:S(2)}) %collective-permute-start) | collective-permute-done | bytes 1179680 | tf_op jit(solution)/shard_map/ppermute | solution.py:13
  187.6 1.1 fusion.7
  188.7 4.6 %collective-permute-start.1 = (f32[576,512]{1,0:T(8,128)S(1)}, f32[576,512]{1,0:T(8,128)S(1)}, u32[]{:S(2)}, u32[]{:S(2)}) collective-permute-start(f32[576,512]{1,0:T(8,128)S(1)} %fusion.7), channel_id=1, source_target_pairs={{0,2},{1,3},{2,0},{3,1},{4,6},{5,7},{6,4},{7,5},{8,10},{9,11},{10,... | collective-permute-start | bytes 3538952 | tf_op jit(solution)/shard_map/ppermute | solution.py:13
  193.3 19.6 %collective-permute-done.3 = f32[576,512]{1,0:T(8,128)S(1)} collective-permute-done((f32[576,512]{1,0:T(8,128)S(1)}, f32[576,512]{1,0:T(8,128)S(1)}, u32[]{:S(2)}, u32[]{:S(2)}) %collective-permute-start.3) | collective-permute-done | bytes 1179680 | tf_op jit(solution)/shard_map/ppermute | solution.py:13
  212.9 1.1 fusion.3
  214.0 4.6 %collective-permute-start.4 = (f32[576,512]{1,0:T(8,128)S(1)}, f32[576,512]{1,0:T(8,128)S(1)}, u32[]{:S(2)}, u32[]{:S(2)}) collective-permute-start(f32[576,512]{1,0:T(8,128)S(1)} %fusion.3), channel_id=1, source_target_pairs={{0,2},{1,3},{2,0},{3,1},{4,6},{5,7},{6,4},{7,5},{8,10},{9,11},{10,... | collective-permute-start | bytes 3538952 | tf_op jit(solution)/shard_map/ppermute | solution.py:13
  218.6 21.7 %collective-permute-done.1 = f32[576,512]{1,0:T(8,128)S(1)} collective-permute-done((f32[576,512]{1,0:T(8,128)S(1)}, f32[576,512]{1,0:T(8,128)S(1)}, u32[]{:S(2)}, u32[]{:S(2)}) %collective-permute-start.1) | collective-permute-done | bytes 1179680 | tf_op jit(solution)/shard_map/ppermute | solution.py:13
  240.3 1.1 fusion.5
  241.4 5.0 %collective-permute-start.2 = (f32[576,512]{1,0:T(8,128)S(1)}, f32[576,512]{1,0:T(8,128)S(1)}, u32[]{:S(2)}, u32[]{:S(2)}) collective-permute-start(f32[576,512]{1,0:T(8,128)S(1)} %fusion.5), channel_id=1, source_target_pairs={{0,4},{1,5},{2,6},{3,7},{4,0},{5,1},{6,2},{7,3},{8,12},{9,13},{10,... | collective-permute-start | bytes 3538952 | tf_op jit(solution)/shard_map/ppermute | solution.py:13
  246.4 17.7 %collective-permute-done.4 = f32[576,512]{1,0:T(8,128)S(1)} collective-permute-done((f32[576,512]{1,0:T(8,128)S(1)}, f32[576,512]{1,0:T(8,128)S(1)}, u32[]{:S(2)}, u32[]{:S(2)}) %collective-permute-start.4) | collective-permute-done | bytes 1179680 | tf_op jit(solution)/shard_map/ppermute | solution.py:13
  264.2 1.1 fusion.1
  265.3 5.2 %collective-permute-start.5 = (f32[576,512]{1,0:T(8,128)S(1)}, f32[576,512]{1,0:T(8,128)S(1)}, u32[]{:S(2)}, u32[]{:S(2)}) collective-permute-start(f32[576,512]{1,0:T(8,128)S(1)} %fusion.1), channel_id=1, source_target_pairs={{0,4},{1,5},{2,6},{3,7},{4,0},{5,1},{6,2},{7,3},{8,12},{9,13},{10,... | collective-permute-start | bytes 3538952 | tf_op jit(solution)/shard_map/ppermute | solution.py:13
  270.5 52.0 %collective-permute-done.2 = f32[576,512]{1,0:T(8,128)S(1)} collective-permute-done((f32[576,512]{1,0:T(8,128)S(1)}, f32[576,512]{1,0:T(8,128)S(1)}, u32[]{:S(2)}, u32[]{:S(2)}) %collective-permute-start.2) | collective-permute-done | bytes 1179680 | tf_op jit(solution)/shard_map/ppermute | solution.py:13
  322.5 0.2 add_bitcast_fusion.1
  322.8 24.8 %collective-permute-done.5 = f32[576,512]{1,0:T(8,128)S(1)} collective-permute-done((f32[576,512]{1,0:T(8,128)S(1)}, f32[576,512]{1,0:T(8,128)S(1)}, u32[]{:S(2)}, u32[]{:S(2)}) %collective-permute-start.5) | collective-permute-done | bytes 1179680 | tf_op jit(solution)/shard_map/ppermute | solution.py:13
  347.6 0.2 add_bitcast_fusion
  347.8 1.6 maximum_bitcast_fusion
  (10 shorter events, 0.1 us)
Async XLA Ops:
  7.2 5.4 %copy-start = (bf16[1,1,128,512]{3,2,1,0:T(8,128)(2,1)S(1)}, bf16[1,1,128,512]{3,2,1,0:T(8,128)(2,1)}, u32[]{:S(2)}) copy-start(bf16[1,1,128,512]{3,2,1,0:T(8,128)(2,1)} %param.14) | copy-start | bytes 393220
  7.2 4.4 %copy-start.6 = (s32[1,1,128]{2,1,0:T(1,128)S(1)}, s32[1,1,128]{2,1,0:T(1,128)}, u32[]{:S(2)}) copy-start(s32[1,1,128]{2,1,0:T(1,128)} %param.13) | copy-start | bytes 1540
  7.2 51.7 %all-gather.2.cloned.1.call-start = ((), (), s32[]{:S(2)}) async-start(), calls=%async_computation | async-start | bytes 2949120 | tf_op jit(solution)/shard_map/all_gather | solution.py:77
  10.6 1.9 copy-start.4
  11.6 143.6 %all-reduce.3.cloned.1.call-start = ((), (), s32[]{:S(2)}) async-start(), calls=%async_computation.1 | async-start | bytes 4718592 | tf_op jit(solution)/shard_map/psum | solution.py:85
  14.0 47.8 %copy-start.3 = (bf16[576,1,1,128]{3,0,2,1:T(8,128)(2,1)S(1)}, bf16[576,1,1,128]{3,0,2,1:T(8,128)(2,1)}, u32[]{:S(2)}) copy-start(bf16[576,1,1,128]{3,0,2,1:T(8,128)(2,1)} %param.12) | copy-start | bytes 442372
  14.0 47.8 %copy-start.5 = (f32[1,1,128]{2,1,0:T(1,128)S(1)}, f32[1,1,128]{2,1,0:T(1,128)}, u32[]{:S(2)}) copy-start(f32[1,1,128]{2,1,0:T(1,128)} %param.10) | copy-start | bytes 1540
  67.9 87.3 %copy-start.1 = (bf16[1,3,512,512]{3,2,1,0:T(8,128)(2,1)S(1)}, bf16[1,3,512,512]{3,2,1,0:T(8,128)(2,1)}, u32[]{:S(2)}) copy-start(bf16[1,3,512,512]{3,2,1,0:T(8,128)(2,1)} %param.15) | copy-start | bytes 4718596
  155.2 5.6 %copy-start.2 = (f32[576,512]{1,0:T(8,128)S(1)}, f32[576,512]{1,0:T(8,128)}, u32[]{:S(2)}) copy-start(f32[576,512]{1,0:T(8,128)} %get-tuple-element.28) | copy-start | bytes 3538948
  157.7 29.9 %collective-permute-start = (f32[576,512]{1,0:T(8,128)S(1)}, f32[576,512]{1,0:T(8,128)S(1)}, u32[]{:S(2)}, u32[]{:S(2)}) collective-permute-start(f32[576,512]{1,0:T(8,128)S(1)} %fusion.15), channel_id=1, source_target_pairs={{0,1},{1,0},{2,3},{3,2},{4,5},{5,4},{6,7},{7,6},{8,9},{9,8},{10,11... | collective-permute-start | bytes 3538952 | tf_op jit(solution)/shard_map/ppermute | solution.py:13
  161.9 51.0 %collective-permute-start.3 = (f32[576,512]{1,0:T(8,128)S(1)}, f32[576,512]{1,0:T(8,128)S(1)}, u32[]{:S(2)}, u32[]{:S(2)}) collective-permute-start(f32[576,512]{1,0:T(8,128)S(1)} %fusion.13), channel_id=1, source_target_pairs={{0,1},{1,0},{2,3},{3,2},{4,5},{5,4},{6,7},{7,6},{8,9},{9,8},{10,11... | collective-permute-start | bytes 3538952 | tf_op jit(solution)/shard_map/ppermute | solution.py:13
  188.7 51.6 %collective-permute-start.1 = (f32[576,512]{1,0:T(8,128)S(1)}, f32[576,512]{1,0:T(8,128)S(1)}, u32[]{:S(2)}, u32[]{:S(2)}) collective-permute-start(f32[576,512]{1,0:T(8,128)S(1)} %fusion.7), channel_id=1, source_target_pairs={{0,2},{1,3},{2,0},{3,1},{4,6},{5,7},{6,4},{7,5},{8,10},{9,11},{10,... | collective-permute-start | bytes 3538952 | tf_op jit(solution)/shard_map/ppermute | solution.py:13
  214.0 50.1 %collective-permute-start.4 = (f32[576,512]{1,0:T(8,128)S(1)}, f32[576,512]{1,0:T(8,128)S(1)}, u32[]{:S(2)}, u32[]{:S(2)}) collective-permute-start(f32[576,512]{1,0:T(8,128)S(1)} %fusion.3), channel_id=1, source_target_pairs={{0,2},{1,3},{2,0},{3,1},{4,6},{5,7},{6,4},{7,5},{8,10},{9,11},{10,... | collective-permute-start | bytes 3538952 | tf_op jit(solution)/shard_map/ppermute | solution.py:13
  241.4 81.1 %collective-permute-start.2 = (f32[576,512]{1,0:T(8,128)S(1)}, f32[576,512]{1,0:T(8,128)S(1)}, u32[]{:S(2)}, u32[]{:S(2)}) collective-permute-start(f32[576,512]{1,0:T(8,128)S(1)} %fusion.5), channel_id=1, source_target_pairs={{0,4},{1,5},{2,6},{3,7},{4,0},{5,1},{6,2},{7,3},{8,12},{9,13},{10,... | collective-permute-start | bytes 3538952 | tf_op jit(solution)/shard_map/ppermute | solution.py:13
  265.3 82.3 %collective-permute-start.5 = (f32[576,512]{1,0:T(8,128)S(1)}, f32[576,512]{1,0:T(8,128)S(1)}, u32[]{:S(2)}, u32[]{:S(2)}) collective-permute-start(f32[576,512]{1,0:T(8,128)S(1)} %fusion.1), channel_id=1, source_target_pairs={{0,4},{1,5},{2,6},{3,7},{4,0},{5,1},{6,2},{7,3},{8,12},{9,13},{10,... | collective-permute-start | bytes 3538952 | tf_op jit(solution)/shard_map/ppermute | solution.py:13
Sparse Core Ops, SparseCore 0:
  11.7 47.2 all-gather.1
  68.1 87.1 all-reduce.2
where the time goes:
time: 357 us; the launch traced here: 356 us
  waiting for transfers between devices  292 us (82%)
  starting transfers between devices  24.8 us (7%)
  matrix products  14.4 us (4%)
  between operations  14.3 us (4%)
  local copies, waits for them, and re-layouts  7.42 us (2%)
  other arithmetic  3.81 us (1%)
    ppermute x6, waiting for transfers between devices, partner(): return lax.ppermute(value, axis, pairs)  159 us
    psum x1, waiting for transfers between devices, shards(): sketch_sum, probe_sum = lax.psum((sketch_part, probe_part), 'blk')  87.3 us
    all_gather x1, waiting for transfers between devices, shards(): piece = lax.all_gather(outgoing, 'blk', axis=1, tiled=True)  44.9 us
    ppermute x6, starting transfers between devices, partner(): return lax.ppermute(value, axis, pairs)  24.7 us
    dot_general x6, matrix products, project(): jnp.dot(current, level_mat.astype(jnp.float32), precision=lax.Precision.H...  7.99 us
  transfers between devices with their start and end apart: 8, of which 8 were waited for; matrix products, arithmetic and copies ran while one was open for 2% of the time, Pallas kernels for 0%

commit v1 on v0

--- a/solution.py
+++ b/solution.py
@@ -74,7 +74,16 @@
         jnp.take(probe_flat, sorting, axis=1), basis_flat, preferred_element_type=jnp.float32
     )
     outgoing = jnp.concatenate([coords, area_row, scaled.astype(jnp.float32)], axis=0)
-    piece = lax.all_gather(outgoing, "blk", axis=1, tiled=True)
+    remake_wires = lambda raw: jnp.concatenate(
+        lax.all_to_all(
+            jnp.stack([raw for _ in range(lax.psum(1, "blk"))], 0),
+            split_axis=0,
+            axis_name="blk",
+            concat_axis=0,
+        ),
+        1,
+    )
+    piece = remake_wires(outgoing)
     near_sum = near_block(coords, area_row[0], piece[:3], piece[3], piece[4:].astype(jnp.bfloat16))
     offdiag = (full_sketch.reshape(probe_count, panels).astype(jnp.float32) - near_sum).astype(
         jnp.bfloat16

time: 357 us -> 369 us (1.034)
  starting transfers between devices: 24.8 us -> 34.3 us
  waiting for transfers between devices: 292 us -> 298 us
    all_to_all x0 -> x1, waiting for transfers between devices: none -> 50.3 us  [shards(): lax.all_to_all(jnp.stack([raw for _ in range(lax.psum(1, 'blk'))], 0), sp...]
    all_gather x1 -> x0, waiting for transfers between devices: 44.9 us -> none  [shards(): piece = lax.all_gather(outgoing, 'blk', axis=1, tiled=True)]
    all_to_all x0 -> x1, starting transfers between devices: none -> 9.59 us  [shards(): lax.all_to_all(jnp.stack([raw for _ in range(lax.psum(1, 'blk'))], 0), sp...]
where the time goes in v1:
time: 369 us; the launch traced here: 368 us
  waiting for transfers between devices  298 us (81%)
  starting transfers between devices  34.3 us (9%)
  between operations  14.2 us (4%)
  matrix products  12.3 us (3%)
  local copies, waits for them, and re-layouts  6.4 us (2%)
    ppermute x6, waiting for transfers between devices, partner(): return lax.ppermute(value, axis, pairs)  159 us
    psum x1, waiting for transfers between devices, shards(): sketch_sum, probe_sum = lax.psum((sketch_part, probe_part), 'blk')  88.2 us
    all_to_all x1, waiting for transfers between devices, shards(): lax.all_to_all(jnp.stack([raw for _ in range(lax.psum(1, 'blk'))], 0), sp...  50.3 us
    ppermute x6, starting transfers between devices, partner(): return lax.ppermute(value, axis, pairs)  24.7 us
    all_to_all x1, starting transfers between devices, shards(): lax.all_to_all(jnp.stack([raw for _ in range(lax.psum(1, 'blk'))], 0), sp...  9.59 us
    dot_general x6, matrix products, project(): jnp.dot(current, level_mat.astype(jnp.float32), precision=lax.Precision.H...  7.98 us
  transfers between devices with their start and end apart: 8, of which 8 were waited for; matrix products, arithmetic and copies ran while one was open for 2% of the time, Pallas kernels for 0%

profile of v1, /device:TPU:25, one launch (start us, length us, event | category | flops | bytes accessed | tf_op | source)
XLA Modules:
  0.0 368.1 jit_solution(2840150175996468157)
XLA Ops:
  7.2 0.0 copy-start
  7.2 1.1 copy.20
  8.3 0.8 copy.19
  9.1 0.8 copy.21
  9.8 0.7 fusion.39
  10.6 0.2 pad_maximum_fusion
  10.8 0.2 copy.22
  10.9 1.6 stack.8
  12.5 9.6 %all-to-all-start = ((f32[8,580,128]{2,1,0:T(8,128)}), f32[8,580,128]{2,1,0:T(8,128)S(1)}, u32[]{:S(2)}, u32[]{:S(2)}) async-start(f32[8,580,128]{2,1,0:T(8,128)} %stack.8), calls=%async_computation | async-start | bytes 4784128 | tf_op jit(solution)/shard_map/all_to_all | solution.py:78
  22.1 0.0 all-reduce.3.cloned.1.call-start
  22.1 0.0 copy-done.6
  22.2 0.0 copy-start.3
  22.2 0.0 copy-start.5
  22.2 0.9 gather_fusion.1
  23.1 0.0 copy-done.4
  23.1 0.0 copy-done
  23.1 1.4 fusion.40
  24.5 50.3 %all-to-all-done = f32[8,580,128]{2,1,0:T(8,128)S(1)} async-done(((f32[8,580,128]{2,1,0:T(8,128)}), f32[8,580,128]{2,1,0:T(8,128)S(1)}, u32[]{:S(2)}, u32[]{:S(2)}) %all-to-all-start) | async-done | bytes 2375712 | tf_op jit(solution)/shard_map/all_to_all | solution.py:78
  74.9 0.0 copy-done.3
  74.9 0.0 copy-done.5
  74.9 1.4 fusion.26
  76.3 0.2 copy.24
  76.5 0.9 gather_fusion
  77.4 1.5 fusion.42
  78.8 0.0 all-reduce.3.cloned.1.call-update
  78.8 88.2 %all-reduce.3.cloned.1.call-done = (f32[576,512]{1,0:T(8,128)}, f32[576,512]{1,0:T(8,128)}) async-done(((f32[576,512]{1,0:T(8,128)}, f32[576,512]{1,0:T(8,128)}), (f32[576,512]{1,0:T(8,128)}, f32[576,512]{1,0:T(8,128)})) %all-reduce.3.cloned.1.call-update) | async-done | bytes 2359312 | tf_op jit(solution)/shard_map/psum | solution.py:94
  167.0 0.0 copy-done.1
  167.0 2.5 fusion.18
  169.5 3.1 collective-permute-start
  172.6 1.1 fusion.16
  173.7 2.2 collective-permute-start.3
  175.9 23.5 %collective-permute-done = f32[576,512]{1,0:T(8,128)S(1)} collective-permute-done((f32[576,512]{1,0:T(8,128)S(1)}, f32[576,512]{1,0:T(8,128)S(1)}, u32[]{:S(2)}, u32[]{:S(2)}) %collective-permute-start) | collective-permute-done | bytes 1179680 | tf_op jit(solution)/shard_map/ppermute | solution.py:13
  199.4 1.1 fusion.10
  200.6 4.6 %collective-permute-start.1 = (f32[576,512]{1,0:T(8,128)S(1)}, f32[576,512]{1,0:T(8,128)S(1)}, u32[]{:S(2)}, u32[]{:S(2)}) collective-permute-start(f32[576,512]{1,0:T(8,128)S(1)} %fusion.10), channel_id=1, source_target_pairs={{0,2},{1,3},{2,0},{3,1},{4,6},{5,7},{6,4},{7,5},{8,10},{9,11},{10,... | collective-permute-start | bytes 3538952 | tf_op jit(solution)/shard_map/ppermute | solution.py:13
  205.2 19.6 %collective-permute-done.3 = f32[576,512]{1,0:T(8,128)S(1)} collective-permute-done((f32[576,512]{1,0:T(8,128)S(1)}, f32[576,512]{1,0:T(8,128)S(1)}, u32[]{:S(2)}, u32[]{:S(2)}) %collective-permute-start.3) | collective-permute-done | bytes 1179680 | tf_op jit(solution)/shard_map/ppermute | solution.py:13
  224.7 1.1 fusion.6
  225.9 4.6 %collective-permute-start.4 = (f32[576,512]{1,0:T(8,128)S(1)}, f32[576,512]{1,0:T(8,128)S(1)}, u32[]{:S(2)}, u32[]{:S(2)}) collective-permute-start(f32[576,512]{1,0:T(8,128)S(1)} %fusion.6), channel_id=1, source_target_pairs={{0,2},{1,3},{2,0},{3,1},{4,6},{5,7},{6,4},{7,5},{8,10},{9,11},{10,... | collective-permute-start | bytes 3538952 | tf_op jit(solution)/shard_map/ppermute | solution.py:13
  230.5 21.7 %collective-permute-done.1 = f32[576,512]{1,0:T(8,128)S(1)} collective-permute-done((f32[576,512]{1,0:T(8,128)S(1)}, f32[576,512]{1,0:T(8,128)S(1)}, u32[]{:S(2)}, u32[]{:S(2)}) %collective-permute-start.1) | collective-permute-done | bytes 1179680 | tf_op jit(solution)/shard_map/ppermute | solution.py:13
  252.1 1.1 fusion.8
  253.2 5.0 %collective-permute-start.2 = (f32[576,512]{1,0:T(8,128)S(1)}, f32[576,512]{1,0:T(8,128)S(1)}, u32[]{:S(2)}, u32[]{:S(2)}) collective-permute-start(f32[576,512]{1,0:T(8,128)S(1)} %fusion.8), channel_id=1, source_target_pairs={{0,4},{1,5},{2,6},{3,7},{4,0},{5,1},{6,2},{7,3},{8,12},{9,13},{10,... | collective-permute-start | bytes 3538952 | tf_op jit(solution)/shard_map/ppermute | solution.py:13
  258.3 17.7 %collective-permute-done.4 = f32[576,512]{1,0:T(8,128)S(1)} collective-permute-done((f32[576,512]{1,0:T(8,128)S(1)}, f32[576,512]{1,0:T(8,128)S(1)}, u32[]{:S(2)}, u32[]{:S(2)}) %collective-permute-start.4) | collective-permute-done | bytes 1179680 | tf_op jit(solution)/shard_map/ppermute | solution.py:13
  276.0 1.1 fusion.4
  277.1 5.2 %collective-permute-start.5 = (f32[576,512]{1,0:T(8,128)S(1)}, f32[576,512]{1,0:T(8,128)S(1)}, u32[]{:S(2)}, u32[]{:S(2)}) collective-permute-start(f32[576,512]{1,0:T(8,128)S(1)} %fusion.4), channel_id=1, source_target_pairs={{0,4},{1,5},{2,6},{3,7},{4,0},{5,1},{6,2},{7,3},{8,12},{9,13},{10,... | collective-permute-start | bytes 3538952 | tf_op jit(solution)/shard_map/ppermute | solution.py:13
  282.3 52.0 %collective-permute-done.2 = f32[576,512]{1,0:T(8,128)S(1)} collective-permute-done((f32[576,512]{1,0:T(8,128)S(1)}, f32[576,512]{1,0:T(8,128)S(1)}, u32[]{:S(2)}, u32[]{:S(2)}) %collective-permute-start.2) | collective-permute-done | bytes 1179680 | tf_op jit(solution)/shard_map/ppermute | solution.py:13
  334.3 0.2 add_bitcast_fusion.1
  334.6 24.8 %collective-permute-done.5 = f32[576,512]{1,0:T(8,128)S(1)} collective-permute-done((f32[576,512]{1,0:T(8,128)S(1)}, f32[576,512]{1,0:T(8,128)S(1)}, u32[]{:S(2)}, u32[]{:S(2)}) %collective-permute-start.5) | collective-permute-done | bytes 1179680 | tf_op jit(solution)/shard_map/ppermute | solution.py:13
  359.4 0.2 add_bitcast_fusion
  359.7 1.6 maximum_bitcast_fusion
  (11 shorter events, 0.1 us)
Async XLA Ops:
  7.2 15.9 %copy-start = (bf16[1,1,128,512]{3,2,1,0:T(8,128)(2,1)S(1)}, bf16[1,1,128,512]{3,2,1,0:T(8,128)(2,1)}, u32[]{:S(2)}) copy-start(bf16[1,1,128,512]{3,2,1,0:T(8,128)(2,1)} %param.14) | copy-start | bytes 393220
  12.5 9.6 %copy-start.6 = (s32[1,1,128]{2,1,0:T(1,128)S(1)}, s32[1,1,128]{2,1,0:T(1,128)}, u32[]{:S(2)}) copy-start(s32[1,1,128]{2,1,0:T(1,128)} %param.13) | copy-start | bytes 1540
  12.5 62.3 %all-to-all-start = ((f32[8,580,128]{2,1,0:T(8,128)}), f32[8,580,128]{2,1,0:T(8,128)S(1)}, u32[]{:S(2)}, u32[]{:S(2)}) async-start(f32[8,580,128]{2,1,0:T(8,128)} %stack.8), calls=%async_computation | async-start | bytes 4784128 | tf_op jit(solution)/shard_map/all_to_all | solution.py:78
  22.1 1.0 copy-start.4
  22.1 144.9 %all-reduce.3.cloned.1.call-start = ((), (), s32[]{:S(2)}) async-start(), calls=%async_computation.1 | async-start | bytes 4718592 | tf_op jit(solution)/shard_map/psum | solution.py:94
  22.2 52.7 %copy-start.3 = (bf16[576,1,1,128]{3,0,2,1:T(8,128)(2,1)S(1)}, bf16[576,1,1,128]{3,0,2,1:T(8,128)(2,1)}, u32[]{:S(2)}) copy-start(bf16[576,1,1,128]{3,0,2,1:T(8,128)(2,1)} %param.12) | copy-start | bytes 442372
  22.2 52.7 %copy-start.5 = (f32[1,1,128]{2,1,0:T(1,128)S(1)}, f32[1,1,128]{2,1,0:T(1,128)}, u32[]{:S(2)}) copy-start(f32[1,1,128]{2,1,0:T(1,128)} %param.10) | copy-start | bytes 1540
  78.8 88.2 %copy-start.1 = (bf16[1,3,512,512]{3,2,1,0:T(8,128)(2,1)S(1)}, bf16[1,3,512,512]{3,2,1,0:T(8,128)(2,1)}, u32[]{:S(2)}) copy-start(bf16[1,3,512,512]{3,2,1,0:T(8,128)(2,1)} %param.15) | copy-start | bytes 4718596
  167.0 5.6 %copy-start.2 = (f32[576,512]{1,0:T(8,128)S(1)}, f32[576,512]{1,0:T(8,128)}, u32[]{:S(2)}) copy-start(f32[576,512]{1,0:T(8,128)} %get-tuple-element.17) | copy-start | bytes 3538948
  169.5 29.9 %collective-permute-start = (f32[576,512]{1,0:T(8,128)S(1)}, f32[576,512]{1,0:T(8,128)S(1)}, u32[]{:S(2)}, u32[]{:S(2)}) collective-permute-start(f32[576,512]{1,0:T(8,128)S(1)} %fusion.18), channel_id=1, source_target_pairs={{0,1},{1,0},{2,3},{3,2},{4,5},{5,4},{6,7},{7,6},{8,9},{9,8},{10,11... | collective-permute-start | bytes 3538952 | tf_op jit(solution)/shard_map/ppermute | solution.py:13
  173.7 51.0 %collective-permute-start.3 = (f32[576,512]{1,0:T(8,128)S(1)}, f32[576,512]{1,0:T(8,128)S(1)}, u32[]{:S(2)}, u32[]{:S(2)}) collective-permute-start(f32[576,512]{1,0:T(8,128)S(1)} %fusion.16), channel_id=1, source_target_pairs={{0,1},{1,0},{2,3},{3,2},{4,5},{5,4},{6,7},{7,6},{8,9},{9,8},{10,11... | collective-permute-start | bytes 3538952 | tf_op jit(solution)/shard_map/ppermute | solution.py:13
  200.6 51.6 %collective-permute-start.1 = (f32[576,512]{1,0:T(8,128)S(1)}, f32[576,512]{1,0:T(8,128)S(1)}, u32[]{:S(2)}, u32[]{:S(2)}) collective-permute-start(f32[576,512]{1,0:T(8,128)S(1)} %fusion.10), channel_id=1, source_target_pairs={{0,2},{1,3},{2,0},{3,1},{4,6},{5,7},{6,4},{7,5},{8,10},{9,11},{10,... | collective-permute-start | bytes 3538952 | tf_op jit(solution)/shard_map/ppermute | solution.py:13
  225.9 50.1 %collective-permute-start.4 = (f32[576,512]{1,0:T(8,128)S(1)}, f32[576,512]{1,0:T(8,128)S(1)}, u32[]{:S(2)}, u32[]{:S(2)}) collective-permute-start(f32[576,512]{1,0:T(8,128)S(1)} %fusion.6), channel_id=1, source_target_pairs={{0,2},{1,3},{2,0},{3,1},{4,6},{5,7},{6,4},{7,5},{8,10},{9,11},{10,... | collective-permute-start | bytes 3538952 | tf_op jit(solution)/shard_map/ppermute | solution.py:13
  253.2 81.1 %collective-permute-start.2 = (f32[576,512]{1,0:T(8,128)S(1)}, f32[576,512]{1,0:T(8,128)S(1)}, u32[]{:S(2)}, u32[]{:S(2)}) collective-permute-start(f32[576,512]{1,0:T(8,128)S(1)} %fusion.8), channel_id=1, source_target_pairs={{0,4},{1,5},{2,6},{3,7},{4,0},{5,1},{6,2},{7,3},{8,12},{9,13},{10,... | collective-permute-start | bytes 3538952 | tf_op jit(solution)/shard_map/ppermute | solution.py:13
  277.1 82.3 %collective-permute-start.5 = (f32[576,512]{1,0:T(8,128)S(1)}, f32[576,512]{1,0:T(8,128)S(1)}, u32[]{:S(2)}, u32[]{:S(2)}) collective-permute-start(f32[576,512]{1,0:T(8,128)S(1)} %fusion.4), channel_id=1, source_target_pairs={{0,4},{1,5},{2,6},{3,7},{4,0},{5,1},{6,2},{7,3},{8,12},{9,13},{10,... | collective-permute-start | bytes 3538952 | tf_op jit(solution)/shard_map/ppermute | solution.py:13
Sparse Core Ops, SparseCore 0:
  79.0 88.0 all-reduce.2
